TPU v7x, 256 devices: a whole 4x4x8 slice. The times are simulated.
256 devices in a mesh: wide: 16 (over y_lo, z), row: 16 (over y_hi, x, core).
Axes of the slice: x: 4, y: 4 (y_hi: 2, y_lo: 2; y = y_hi * 2 + y_lo), z: 8, core: 2. Of those that a mesh axis runs over, the one named last changes fastest.
Arguments:
- hessian: float32 [18432, 18432], P('row', 'wide'), as said below
- weight: bfloat16 [4608, 18432], P('row', 'wide'), may hold values from -6 to 6
- pairs: int32 [2], replicated, may hold values from 0 to 47, as said below
Outputs:
- pruned_hessian: float32 [18432, 18432], P('row', 'wide')
- pruned_weight: bfloat16 [4608, 18432], P('row', 'wide')
Inputs may be any that keep to these rules, and one draw needn't show every extreme that they name: Two different head pairs, one of which is the last pair, 47. `hessian`: symmetric positive definite.
All inputs are finite; a program needn't handle non-finite values.
Results may differ from a plain program's by a relative error of at most 0.001.
Values may be sent and summed in bfloat16 or wider, within the bound.
A program may use at most 128 MiB of HBM per device.

v0:
```python
import jax
import jax.numpy as jnp
from jax import lax
from jax.sharding import PartitionSpec as P

HEAD = 192


def broadcast(value, axis, source):
    kept = jnp.where(lax.axis_index(axis) == source, value, 0).astype(value.dtype)
    return lax.psum(kept, axis)


def per_device(hessian, weight, pairs):
    tile_rows, tile_cols = hessian.shape
    pair_width = 2 * HEAD
    row_here = lax.axis_index("row")
    highest = lax.Precision.HIGHEST
    pair_one = pairs[0]
    pair_two = pairs[1]

    def where_is(pair_index, extent):
        start_col = pair_index * pair_width
        return (start_col // extent, start_col % extent)

    def column_panel(matrix, pair_index):
        holder, offset = where_is(pair_index, tile_cols)
        local_cols = lax.dynamic_slice_in_dim(matrix, offset, pair_width, 1)
        return broadcast(local_cols, "wide", holder)

    def solved_rows(matrix, panel, pair_index):
        holder, offset = where_is(pair_index, tile_rows)
        pivot_block = lax.dynamic_slice_in_dim(panel, offset, pair_width, 0)
        pivot_block = jnp.where(
            row_here == holder, pivot_block, jnp.eye(pair_width, dtype=jnp.float32)
        )
        rows_local = lax.dynamic_slice_in_dim(matrix, offset, pair_width, 0)
        factor = jnp.linalg.cholesky(pivot_block)
        solved = jax.scipy.linalg.cho_solve((factor, True), rows_local)
        return broadcast(solved, "row", holder)

    panel_one = column_panel(hessian, pair_one)
    solved_one = solved_rows(hessian, panel_one, pair_one)
    holder_one, offset_one = where_is(pair_one, tile_cols)
    weight_one = broadcast(
        lax.dynamic_slice_in_dim(weight, offset_one, pair_width, 1), "wide", holder_one
    )
    updated = hessian - jnp.dot(panel_one, solved_one, precision=highest)
    carried = weight.astype(jnp.float32) - jnp.dot(
        weight_one.astype(jnp.float32), solved_one, precision=highest
    )
    panel_two = column_panel(updated, pair_two)
    solved_two = solved_rows(updated, panel_two, pair_two)
    holder_two, offset_two = where_is(pair_two, tile_cols)
    weight_two = broadcast(
        lax.dynamic_slice_in_dim(carried, offset_two, pair_width, 1), "wide", holder_two
    )
    pruned_hessian = updated - jnp.dot(panel_two, solved_two, precision=highest)
    pruned_weight = (carried - jnp.dot(weight_two, solved_two, precision=highest)).astype(
        jnp.bfloat16
    )
    return (pruned_hessian, pruned_weight)


def solution(mesh):
    return jax.shard_map(
        per_device,
        mesh=mesh,
        in_specs=(P("row", "wide"), P("row", "wide"), P()),
        out_specs=(P("row", "wide"), P("row", "wide")),
        check_vma=False,
    )
```

profile of v0, /device:TPU:7, one launch (start us, length us, event | category | flops | bytes accessed | tf_op | source)
XLA Modules:
  0.0 914.7 jit_solution(16918178659369243016)
XLA Ops:
  7.2 1.3 fusion.59
  9.2 6.9 copy.7
  16.1 2.9 dynamic-slice_select_fusion.1
  19.0 1.8 dynamic-slice_select_fusion.3
  20.9 131.7 %all-reduce.8.cloned.1.call-done = f32[1152,384]{0,1:T(8,128)} async-done(((f32[1152,384]{0,1:T(8,128)}), f32[1152,384]{0,1:T(8,128)}) %all-reduce.8.cloned.1.call-update) | async-done | bytes 1769488 | tf_op jit(solution)/shard_map/psum | solution.py:11
  152.6 1.4 convert_select_fusion.1
  154.5 11.7 %cholesky.208 = f32[128,128]{1,0:T(8,128)S(1)} custom-call(f32[128,128]{1,0:T(8,128)S(1)} %cholesky.310), custom_call_target="Cholesky" | custom-call | tf_op jit(solution)/shard_map/jit(cholesky)/cholesky | solution.py:38
  166.2 9.8 %custom-call.22 = f32[1,128,128]{1,2,0:T(8,128)S(1)} custom-call(f32[1,128,128]{2,1,0:T(8,128)S(1)} %get-tuple-element.57), custom_call_target="InvertDiagBlocksLowerTriangular" | custom-call | tf_op jit(solution)/shard_map/jit(cholesky)/cholesky | solution.py:38
  176.6 11.7 %cholesky.227 = f32[128,128]{1,0:T(8,128)S(1)} custom-call(f32[128,128]{1,0:T(8,128)S(1)} %cholesky.314), custom_call_target="Cholesky" | custom-call | tf_op jit(solution)/shard_map/jit(cholesky)/cholesky | solution.py:38
  188.4 10.0 %custom-call.23 = f32[1,128,128]{1,2,0:T(8,128)S(1)} custom-call(f32[1,128,128]{2,1,0:T(8,128)S(1)} %get-tuple-element.54), custom_call_target="InvertDiagBlocksLowerTriangular" | custom-call | tf_op jit(solution)/shard_map/jit(cholesky)/cholesky | solution.py:38
  198.8 11.7 %cholesky.246 = f32[128,128]{1,0:T(8,128)S(1)} custom-call(f32[128,128]{1,0:T(8,128)S(1)} %convolution_subtract_fusion.15), custom_call_target="Cholesky" | custom-call | tf_op jit(solution)/shard_map/jit(cholesky)/cholesky | solution.py:38
  214.0 6.1 while.4
  214.6 1.3 bitcast_dynamic-update-slice_fusion.4
  216.7 1.3 bitcast_dynamic-update-slice_fusion.4
  218.7 1.3 bitcast_dynamic-update-slice_fusion.4
  220.1 29.5 %custom-call.24 = f32[3,128,128]{1,2,0:T(8,128)S(1)} custom-call(f32[3,128,128]{2,1,0:T(8,128)S(1)} %get-tuple-element.18), custom_call_target="InvertDiagBlocksLowerTriangular" | custom-call | tf_op jit(solution)/shard_map/jit(_cho_solve)/triangular_solve | solution.py:39
  249.6 1.8 fusion.15
  251.3 1.7 convolution_subtract_fusion.11
  253.8 1.9 convolution_subtract_fusion.10
  262.1 26.1 %all-reduce.14.cloned.1.call-done = bf16[288,384]{1,0:T(8,128)(2,1)} async-done(((bf16[288,384]{1,0:T(8,128)(2,1)}), bf16[288,384]{1,0:T(8,128)(2,1)}) %all-reduce.14.cloned.1.call-update) | async-done | bytes 221200 | tf_op jit(solution)/shard_map/psum | solution.py:11
  288.2 159.2 %all-reduce.10.cloned.1.call-done = f32[384,1152]{1,0:T(8,128)} async-done(((f32[384,1152]{1,0:T(8,128)}), f32[384,1152]{1,0:T(8,128)}) %all-reduce.10.cloned.1.call-update) | async-done | bytes 1769488 | tf_op jit(solution)/shard_map/psum | solution.py:11
  447.4 3.2 convolution_subtract_fusion.2
  451.6 12.4 %convolution_subtract_fusion.1 = f32[1152,1152]{0,1:T(8,128)S(1)} fusion(f32[1152,1152]{0,1:T(8,128)} %copy.7, f32[1152,384]{0,1:T(8,128)S(1)} %copy-done.1, f32[384,1152]{1,0:T(8,128)S(1)} %copy-done.3), kind=kOutput, calls=%fused_computation.5 | convolution fusion | flops 6116622336 | bytes 14155776 | tf_op jit(solution)/shard_map/dot_general | solution.py:48
  464.0 2.4 copy-done
  466.4 1.4 dynamic-slice_select_fusion
  468.0 132.8 %all-reduce.16.cloned.1.call-done = (f32[1152,384]{0,1:T(8,128)}, f32[288,384]{1,0:T(8,128)}) async-done(((f32[1152,384]{0,1:T(8,128)}, f32[288,384]{1,0:T(8,128)}), (f32[1152,384]{0,1:T(8,128)}, f32[288,384]{1,0:T(8,128)})) %all-reduce.16.cloned.1.call-update) | async-done | bytes 2211856 | tf_op jit(solution)/shard_map/psum | solution.py:11
  600.8 2.2 convert_select_fusion
  603.0 2.1 copy.9
  607.3 11.7 %cholesky.261 = f32[128,128]{1,0:T(8,128)S(1)} custom-call(f32[128,128]{1,0:T(8,128)S(1)} %cholesky.318), custom_call_target="Cholesky" | custom-call | tf_op jit(solution)/shard_map/jit(cholesky)/cholesky | solution.py:38
  619.7 9.8 %custom-call.25 = f32[1,128,128]{1,2,0:T(8,128)S(1)} custom-call(f32[1,128,128]{2,1,0:T(8,128)S(1)} %get-tuple-element.50), custom_call_target="InvertDiagBlocksLowerTriangular" | custom-call | tf_op jit(solution)/shard_map/jit(cholesky)/cholesky | solution.py:38
  630.3 1.8 constant_dynamic-update-slice_fusion
  633.3 11.7 %cholesky.280 = f32[128,128]{1,0:T(8,128)S(1)} custom-call(f32[128,128]{1,0:T(8,128)S(1)} %cholesky.322), custom_call_target="Cholesky" | custom-call | tf_op jit(solution)/shard_map/jit(cholesky)/cholesky | solution.py:38
  646.4 10.0 %custom-call.26 = f32[1,128,128]{1,2,0:T(8,128)S(1)} custom-call(f32[1,128,128]{2,1,0:T(8,128)S(1)} %get-tuple-element.47), custom_call_target="InvertDiagBlocksLowerTriangular" | custom-call | tf_op jit(solution)/shard_map/jit(cholesky)/cholesky | solution.py:38
  658.5 11.7 %cholesky.299 = f32[128,128]{1,0:T(8,128)S(1)} custom-call(f32[128,128]{1,0:T(8,128)S(1)} %convolution_subtract_fusion.14), custom_call_target="Cholesky" | custom-call | tf_op jit(solution)/shard_map/jit(cholesky)/cholesky | solution.py:38
  673.5 1.9 select_select_fusion
  675.4 8.5 while.5
  676.1 2.2 bitcast_dynamic-update-slice_fusion.5
  679.0 2.2 bitcast_dynamic-update-slice_fusion.5
  681.8 2.1 bitcast_dynamic-update-slice_fusion.5
  683.9 29.5 %custom-call.27 = f32[3,128,128]{1,2,0:T(8,128)S(1)} custom-call(f32[3,128,128]{2,1,0:T(8,128)S(1)} %get-tuple-element.19), custom_call_target="InvertDiagBlocksLowerTriangular" | custom-call | tf_op jit(solution)/shard_map/jit(_cho_solve)/triangular_solve | solution.py:39
  713.5 2.2 fusion.13
  715.7 2.5 convolution_subtract_fusion.7
  719.0 3.1 convolution_subtract_fusion.6
  726.2 1.3 maximum_select_fusion.1
  727.6 157.2 %all-reduce.12.cloned.1.call-done = f32[384,1152]{1,0:T(8,128)} async-done(((f32[384,1152]{1,0:T(8,128)}), f32[384,1152]{1,0:T(8,128)}) %all-reduce.12.cloned.1.call-update) | async-done | bytes 1769488 | tf_op jit(solution)/shard_map/psum | solution.py:11
  884.7 12.7 %convolution_subtract_fusion = f32[1152,1152]{0,1:T(8,128)} fusion(f32[1152,1152]{0,1:T(8,128)} %copy-done, f32[1152,384]{0,1:T(8,128)S(1)} %copy-done.2, f32[384,1152]{1,0:T(8,128)} %all-reduce.12.cloned.1.call-done), kind=kOutput, calls=%fused_computation.4 | convolution fusion | flops 6116622336 | bytes 14155776 | tf_op jit(solution)/shard_map/dot_general | solution.py:58
  897.4 7.0 copy.11
  904.5 3.3 fusion
  (85 shorter events, 29.3 us)
Async XLA Ops:
  7.2 145.4 %all-reduce.8.cloned.1.call-start = ((), (), s32[]{:S(2)}) async-start(), calls=%async_computation | async-start | bytes 3538944 | tf_op jit(solution)/shard_map/psum | solution.py:11
  19.0 269.3 %all-reduce.14.cloned.1.call-start = ((), (), s32[]{:S(2)}) async-start(), calls=%async_computation.3 | async-start | bytes 442368 | tf_op jit(solution)/shard_map/psum | solution.py:11
  20.8 426.6 %all-reduce.10.cloned.1.call-start = ((), (), s32[]{:S(2)}) async-start(), calls=%async_computation.1 | async-start | bytes 3538944 | tf_op jit(solution)/shard_map/psum | solution.py:11
  152.6 1.7 copy-start.1
  261.1 339.8 %all-reduce.16.cloned.1.call-start = ((), (), s32[]{:S(2)}) async-start(), calls=%async_computation.4 | async-start | bytes 4423680 | tf_op jit(solution)/shard_map/psum | solution.py:11
  447.4 4.1 copy-start.3
  464.0 2.4 copy-start
  467.8 417.0 %all-reduce.12.cloned.1.call-start = ((), (), s32[]{:S(2)}) async-start(), calls=%async_computation.2 | async-start | bytes 3538944 | tf_op jit(solution)/shard_map/psum | solution.py:11
  600.8 4.4 copy-start.2
  606.5 0.8 copy-start.6
  715.7 3.3 copy-start.5
  897.4 7.0 copy-start.4
  897.4 7.0 copy-start.7
Sparse Core Ops, SparseCore 0:
  19.1 133.4 all-reduce.7
  155.8 132.4 all-reduce.13
  290.9 156.4 all-reduce.9
  467.9 132.8 all-reduce.15
  727.7 156.9 all-reduce.11
where the time goes:
time: 925 us; the launch traced here: 915 us
  waiting for transfers between devices  607 us (66%)
  other arithmetic  190 us (21%)
  matrix products  60.4 us (7%)
  local copies, waits for them, and re-layouts  36.2 us (4%)
  between operations  19.7 us (2%)
    psum x5, waiting for transfers between devices, broadcast(): return lax.psum(kept, axis)  607 us
    another operation x21, other arithmetic, solved_rows(): factor = jnp.linalg.cholesky(pivot_block)  115 us
    another operation x5, other arithmetic, solved_rows(): solved = jax.scipy.linalg.cho_solve((factor, True), rows_local)  61 us
    another operation x20, matrix products, solved_rows(): solved = jax.scipy.linalg.cho_solve((factor, True), rows_local)  22.8 us
  transfers between devices with their start and end apart: 5, of which 5 were waited for; matrix products, arithmetic and copies ran while one was open for 12% of the time, Pallas kernels for 0%

commit v1 on v0

--- a/solution.py
+++ b/solution.py
@@ -8,7 +8,7 @@
 
 def broadcast(value, axis, source):
     kept = jnp.where(lax.axis_index(axis) == source, value, 0).astype(value.dtype)
-    return lax.psum(kept, axis)
+    return jnp.sum(lax.all_gather(kept, axis), axis=0)
 
 
 def per_device(hessian, weight, pairs):

time: 925 us -> 1310 us (1.42)
  waiting for transfers between devices: 607 us -> 970 us
  other arithmetic: 190 us -> 234 us
  local copies, waits for them, and re-layouts: 36.2 us -> 18 us
    all_gather x0 -> x6, waiting for transfers between devices: none -> 970 us  [broadcast(): return jnp.sum(lax.all_gather(kept, axis), axis=0)]
    psum x5 -> x0, waiting for transfers between devices: 607 us -> none  [broadcast(): return lax.psum(kept, axis)]
    reduce_sum x0 -> x6, other arithmetic: none -> 50.2 us  [broadcast(): return jnp.sum(lax.all_gather(kept, axis), axis=0)]
    unnamed x18 -> x12, local copies, waits for them, and re-layouts: 17.1 us -> 3.93 us
  transfers between devices with their start and end apart: 5 -> 6, of which waited for: 5 -> 5; matrix products, arithmetic and copies ran while one was open for 12% -> 12% of each run, Pallas kernels for 0% -> 0%
where the time goes in v1:
time: 1310 us; the launch traced here: 1290 us
  waiting for transfers between devices  970 us (74%)
  other arithmetic  234 us (18%)
  matrix products  50.7 us (4%)
  between operations  20.3 us (2%)
  local copies, waits for them, and re-layouts  18 us (1%)
    all_gather x6, waiting for transfers between devices, broadcast(): return jnp.sum(lax.all_gather(kept, axis), axis=0)  970 us
    another operation x21, other arithmetic, solved_rows(): factor = jnp.linalg.cholesky(pivot_block)  113 us
    another operation x5, other arithmetic, solved_rows(): solved = jax.scipy.linalg.cho_solve((factor, True), rows_local)  59.6 us
    reduce_sum x6, other arithmetic, broadcast(): return jnp.sum(lax.all_gather(kept, axis), axis=0)  50.2 us
  transfers between devices with their start and end apart: 6, of which 5 were waited for; matrix products, arithmetic and copies ran while one was open for 12% of the time, Pallas kernels for 0%

profile of v1, /device:TPU:7, one launch (start us, length us, event | category | flops | bytes accessed | tf_op | source)
XLA Modules:
  0.0 1293.3 jit_solution(12046963656399442881)
XLA Ops:
  7.2 1.4 fusion.59
  9.3 3.2 dynamic-slice_select_fusion.1
  12.6 303.9 %all-gather.13.cloned.1.call-done = f32[18432,384]{1,0:T(8,128)} async-done(((f32[1152,384]{1,0:T(8,128)}), f32[18432,384]{1,0:T(8,128)}) %all-gather.13.cloned.1.call-update) | async-done | bytes 28311568 | tf_op jit(solution)/shard_map/all_gather | solution.py:11
  316.5 10.7 reduce_sum.57
  327.9 11.7 cholesky.208
  339.6 9.8 custom-call.22
  350.1 11.7 cholesky.227
  361.8 10.0 custom-call.23
  372.3 11.7 cholesky.246
  387.4 6.0 while.4
  388.0 1.4 bitcast_dynamic-update-slice_fusion.4
  390.0 1.4 bitcast_dynamic-update-slice_fusion.4
  392.0 1.4 bitcast_dynamic-update-slice_fusion.4
  393.4 29.7 %custom-call.24 = f32[3,128,128]{1,2,0:T(8,128)S(1)} custom-call(f32[3,128,128]{2,1,0:T(8,128)S(1)} %get-tuple-element.18), custom_call_target="InvertDiagBlocksLowerTriangular" | custom-call | tf_op jit(solution)/shard_map/jit(_cho_solve)/triangular_solve | solution.py:39
  423.1 1.8 fusion.15
  424.9 1.7 convolution_subtract_fusion.11
  427.3 1.9 convolution_subtract_fusion.10
  433.3 1.3 maximum_select_fusion
  434.7 1.8 dynamic-slice_select_fusion.3
  437.2 162.0 %all-gather.15.cloned.1.call-done = f32[6144,1152]{1,0:T(8,128)} async-done(((f32[384,1152]{1,0:T(8,128)}), f32[6144,1152]{1,0:T(8,128)}) %all-gather.15.cloned.1.call-update) | async-done | bytes 28311568 | tf_op jit(solution)/shard_map/all_gather | solution.py:11
  599.3 11.2 reduce_sum.58
  610.5 11.4 convolution_subtract_fusion.1
  621.9 2.4 copy-done
  624.2 1.7 dynamic-slice_select_fusion
  626.0 40.0 %all-gather.21.cloned.1.call-done = bf16[4608,384]{1,0:T(8,128)(2,1)} async-done(((bf16[288,384]{1,0:T(8,128)(2,1)}), bf16[4608,384]{1,0:T(8,128)(2,1)}) %all-gather.21.cloned.1.call-update) | async-done | bytes 3538960 | tf_op jit(solution)/shard_map/all_gather | solution.py:11
  666.1 2.6 reduce_sum.61
  668.7 1.4 convolution_subtract_fusion.2
  672.2 303.6 %all-gather.17.cloned.1.call-done = f32[18432,384]{1,0:T(8,128)} async-done(((f32[1152,384]{1,0:T(8,128)}), f32[18432,384]{1,0:T(8,128)}) %all-gather.17.cloned.1.call-update) | async-done | bytes 28311568 | tf_op jit(solution)/shard_map/all_gather | solution.py:11
  975.8 10.8 reduce_sum.59
  987.3 11.7 cholesky.261
  999.1 9.8 custom-call.25
  1009.5 11.7 cholesky.280
  1021.2 10.0 custom-call.26
  1031.7 11.7 cholesky.299
  1047.5 6.0 while.5
  1048.2 1.3 bitcast_dynamic-update-slice_fusion.5
  1050.2 1.3 bitcast_dynamic-update-slice_fusion.5
  1052.2 1.3 bitcast_dynamic-update-slice_fusion.5
  1053.6 29.7 %custom-call.27 = f32[3,128,128]{1,2,0:T(8,128)S(1)} custom-call(f32[3,128,128]{2,1,0:T(8,128)S(1)} %get-tuple-element.19), custom_call_target="InvertDiagBlocksLowerTriangular" | custom-call | tf_op jit(solution)/shard_map/jit(_cho_solve)/triangular_solve | solution.py:39
  1083.3 1.8 fusion.13
  1085.1 1.7 convolution_subtract_fusion.7
  1087.5 1.9 convolution_subtract_fusion.6
  1093.4 1.3 maximum_select_fusion.1
  1094.8 4.1 reduce_sum.62
  1099.0 160.5 %all-gather.19.cloned.1.call-done = f32[6144,1152]{1,0:T(8,128)} async-done(((f32[384,1152]{1,0:T(8,128)}), f32[6144,1152]{1,0:T(8,128)}) %all-gather.19.cloned.1.call-update) | async-done | bytes 28311568 | tf_op jit(solution)/shard_map/all_gather | solution.py:11
  1259.4 10.7 reduce_sum.60
  1270.2 12.6 convolution_subtract_fusion
  1282.8 3.3 fusion
  (90 shorter events, 22.8 us)
Async XLA Ops:
  7.2 309.3 %all-gather.13.cloned.1.call-start = ((), (), s32[]{:S(2)}) async-start(), calls=%async_computation | async-start | bytes 30081024 | tf_op jit(solution)/shard_map/all_gather | solution.py:11
  12.5 586.7 %all-gather.15.cloned.1.call-start = ((), (), s32[]{:S(2)}) async-start(), calls=%async_computation.1 | async-start | bytes 30081024 | tf_op jit(solution)/shard_map/all_gather | solution.py:11
  434.6 231.4 %all-gather.21.cloned.1.call-start = ((), (), s32[]{:S(2)}) async-start(), calls=%async_computation.4 | async-start | bytes 3760128 | tf_op jit(solution)/shard_map/all_gather | solution.py:11
  436.4 539.3 %all-gather.17.cloned.1.call-start = ((), (), s32[]{:S(2)}) async-start(), calls=%async_computation.2 | async-start | bytes 30081024 | tf_op jit(solution)/shard_map/all_gather | solution.py:11
  621.8 2.4 copy-start
  626.0 468.8 %all-gather.23.cloned.1.call-start = ((), (), s32[]{:S(2)}) async-start(), calls=%async_computation.5 | async-start | bytes 7520256 | tf_op jit(solution)/shard_map/all_gather | solution.py:11
  666.1 2.7 copy-start.4
  670.1 1.1 copy-start.1
  672.1 587.3 %all-gather.19.cloned.1.call-start = ((), (), s32[]{:S(2)}) async-start(), calls=%async_computation.3 | async-start | bytes 30081024 | tf_op jit(solution)/shard_map/all_gather | solution.py:11
  1270.2 12.6 copy-start.2
  1270.2 12.6 copy-start.3
Sparse Core Ops, SparseCore 0:
  12.7 303.8 all-gather.12
  434.7 164.4 all-gather.14
  601.6 64.3 all-gather.20
  667.7 308.0 all-gather.16
  978.0 85.4 all-gather.22
  1094.9 164.4 all-gather.18
